TPU v7x, 128 devices: a whole 4x4x4 slice. The times are simulated.
128 devices in a mesh: row: 8 (over x_hi, z), col: 8 (over x_lo, y), layer: 2 (over core).
Axes of the slice: x: 4 (x_hi: 2, x_lo: 2; x = x_hi * 2 + x_lo), y: 4, z: 4, core: 2. Of those that a mesh axis runs over, the one named last changes fastest.
Arguments:
- matrix: float32 [32, 512, 32, 512], P('row', None, 'col', 'layer'), may hold values from -40 to 40, as said below
- transforms: float32 [1, 16, 1024, 1024], P(None, 'row', ('col', 'layer')), may hold values from -0.1875 to 0.1875
Outputs:
- swept: float32 [32, 512, 32, 512], P('row', None, 'col', 'layer')
Inputs may be any that keep to these rules, and one draw needn't show every extreme that they name: `matrix`: symmetric: entry [i, a, j, b] equals entry [j, b, i, a].
All inputs are finite; a program needn't handle non-finite values.
Results may differ from a plain program's by a relative error of at most 0.0001.
Values sent between devices are 32-bit elements; how exact they have to be, the bound alone decides.
No kernel may reach another device: no remote copies, remote signals or barrier semaphores. Data moves between devices by JAX's collectives and lax.ppermute only.
A program may use at most 192 MiB of HBM per device.

v0:
```python
import jax
import jax.numpy as jnp
from jax import lax
from jax.sharding import PartitionSpec as P

exact_mode = lax.Precision.HIGHEST


def broadcast(x, axis, root):
    mine = lax.axis_index(axis) == root
    return lax.psum(jnp.where(mine, x, jnp.zeros_like(x)), axis)


def cut_along(x, dim, count):
    before, after = (x.shape[:dim], x.shape[dim + 1 :])
    return jnp.moveaxis(x.reshape(*before, count, -1, *after), dim, 0)


def sum_at_owner(x, axis, dim):
    count = lax.axis_size(axis)
    blocks = lax.all_to_all(cut_along(x, dim, count), axis, 0, 0, tiled=True)
    return jnp.sum(blocks, axis=0)


def passed_along(block, axis, distance):
    devices = range(lax.axis_size(axis))
    route = [(i - distance, i) for i in devices if i - distance in devices]
    return lax.ppermute(block, axis, route)


def split_slots(array, axis_dim):
    return [
        lax.index_in_dim(array, index, axis_dim, keepdims=False)
        for index in range(array.shape[axis_dim])
    ]


def leading(slots):
    width = len(slots)
    return slots[width - 2]


def rearranged(slots, from_prev, from_next, position, count):
    width = len(slots)
    result = [jnp.where(position == 0, slots[0], from_prev)]
    for local in range(1, width):
        if local % 2 == 1:
            if local == width - 1:
                result.append(jnp.where(position == count - 1, slots[width - 2], from_next))
            else:
                result.append(slots[local + 2])
        else:
            result.append(jnp.where(position == 0, slots[1], slots[0]))
    return result


def shards(matrix, transforms):
    pair_dev = matrix.shape[0] // 2
    block_size = matrix.shape[1]
    half_width = matrix.shape[3]
    width = 2 * pair_dev
    pairs_row = lax.axis_size("row")
    pairs_col = lax.axis_size("col")
    row_pos = lax.axis_index("row")
    col_pos = lax.axis_index("col")
    layer_pos = lax.axis_index("layer")
    current = matrix
    left_panel = lax.all_gather(transforms[0], ("col", "layer"), axis=1, tiled=True)
    shaped = left_panel.reshape(pair_dev, 2, block_size, 2 * block_size)
    selected = lax.dynamic_slice_in_dim(shaped, layer_pos * half_width, half_width, 2)
    right_part = broadcast(selected, "row", col_pos)
    grouped = current.reshape(pair_dev, 2 * block_size, width * half_width)
    partial_rows = jnp.einsum(
        "pka,pkc->pac",
        left_panel,
        grouped,
        precision=exact_mode,
        preferred_element_type=jnp.float32,
    )
    partial_rows = partial_rows.reshape(pair_dev, 2 * block_size, pair_dev, 2, half_width)
    term_pairs = jnp.einsum(
        "paqmh,qmhb->paqb",
        partial_rows,
        right_part,
        precision=exact_mode,
        preferred_element_type=jnp.float32,
    )
    term_pairs = term_pairs.reshape(pair_dev, 2 * block_size, pair_dev, 2, 2, half_width)
    rotated = sum_at_owner(term_pairs, "layer", 4)
    rotated = rotated.reshape(width, block_size, width, half_width)
    rows = split_slots(rotated, 0)
    upward = passed_along(leading(rows), "row", 1)
    downward = passed_along(rows[1], "row", -1)
    moved = jnp.stack(rearranged(rows, upward, downward, row_pos, pairs_row), 0)
    cols = split_slots(moved, 2)
    upward_cols = passed_along(leading(cols), "col", 1)
    downward_cols = passed_along(cols[1], "col", -1)
    current = jnp.stack(rearranged(cols, upward_cols, downward_cols, col_pos, pairs_col), 2)
    return current


def solution(mesh):
    return jax.shard_map(
        shards,
        mesh=mesh,
        in_specs=(P("row", None, "col", "layer"), P(None, "row", ("col", "layer"), None)),
        out_specs=P("row", None, "col", "layer"),
        check_vma=False,
    )
```

profile of v0, /device:TPU:120, one launch (start us, length us, event | category | flops | bytes accessed | tf_op | source)
XLA Modules:
  0.0 413.2 jit_solution(15162404626442989335)
XLA Ops:
  6.5 0.7 all-gather.3.cloned.1.call-update
  7.3 0.0 all-reduce.2.cloned.1.call-start
  7.3 54.8 %all-gather.3.cloned.1.call-done = f32[1,2,1024,1024]{3,2,1,0:T(8,128)} async-done(((f32[1,2,64,1024]{3,2,1,0:T(8,128)}), f32[1,2,1024,1024]{3,2,1,0:T(8,128)}) %all-gather.3.cloned.1.call-update) | async-done | bytes 8388624 | tf_op jit(solution)/shard_map/all_gather | solution.py:68
  62.1 4.8 %constant_dynamic-slice_fusion = f32[2,2,256,1024]{3,2,1,0:T(8,128)} fusion(f32[2,2,512,1024]{3,2,1,0:T(8,128)} %bitcast.73, s32[]{:T(128)S(6)} %select_n.56), kind=kLoop, calls=%fused_computation.23 | loop fusion | bytes 8388612 | tf_op jit(solution)/shard_map/dynamic_slice | solution.py:70
  66.9 5.4 %copy.45 = f32[2,2,256,1024]{2,3,1,0:T(8,128)} copy(f32[2,2,256,1024]{3,2,1,0:T(8,128)} %constant_dynamic-slice_fusion) | data formatting | bytes 8388608
  72.3 4.5 %broadcast_select_fusion = f32[2,2,256,1024]{2,3,1,0:T(8,128)} fusion(f32[2,2,256,1024]{2,3,1,0:T(8,128)} %copy.45, pred[]{:T(512)S(6)} %eq.19), kind=kLoop, calls=%fused_computation.20 | loop fusion | flops 1048576 | bytes 8388609 | tf_op jit(solution)/shard_map/jit(_where)/select_n | solution.py:11
  76.9 10.7 %reshape.15 = f32[2,1024,1024]{2,1,0:T(8,128)} reshape(f32[4,512,4,256]{3,2,1,0:T(4,128)} %param.2) | data formatting | bytes 16777216 | tf_op jit(solution)/shard_map/reshape | solution.py:72
  87.6 31.5 %fusion.2 = f32[2,1024,1024]{1,2,0:T(8,128)} fusion(f32[2,1024,1024]{2,1,0:T(8,128)} %reshape.15, f32[1,2,1024,1024]{3,2,1,0:T(8,128)} %all-gather.3.cloned.1.call-done), kind=kOutput, calls=%fused_computation.5 | convolution fusion | flops 25769803776 | bytes 25165824 | tf_op jit(solution)/shard_map/pka,pkc->pac/dot_general | solution.py:73
  119.1 66.1 %all-reduce.2.cloned.1.call-done = f32[2,2,256,1024]{2,3,1,0:T(8,128)} async-done(((f32[2,2,256,1024]{2,3,1,0:T(8,128)}), f32[2,2,256,1024]{2,3,1,0:T(8,128)}) %all-reduce.2.cloned.1.call-update) | async-done | bytes 4194320 | tf_op jit(solution)/shard_map/psum | solution.py:11
  185.2 31.1 %fusion = f32[2,1024,2,1024,1]{3,1,4,2,0:T(8,128)S(1)} fusion(f32[2,1024,2,2,256]{1,4,3,2,0:T(8,128)} %bitcast.72, f32[2,2,256,1024]{2,3,1,0:T(8,128)} %all-reduce.2.cloned.1.call-done), kind=kOutput, calls=%fused_computation.3 | convolution fusion | flops 25769803776 | bytes 29360128 | tf_op jit(solution)/shard_map/paqmh,qmhb->paqb/dot_general | solution.py:81
  216.3 2.9 copy.55
  219.2 19.0 %all_to_all.5 = f32[2,2,1024,2,2,1,256]{2,6,4,1,3,5,0:T(8,128)} all-to-all(f32[2,2,1024,2,2,1,256]{2,6,4,1,3,5,0:T(8,128)S(1)} %bitcast.68), channel_id=1, replica_groups=mesh['row'=8,'col'=8,'layer'=2] {'layer'}, dimensions={0} | all-to-all | bytes 33554432 | tf_op jit(solution)/shard_map/all_to_all | solution.py:21
  238.3 12.2 %reduce_sum.9 = f32[2,1024,2,2,256]{1,4,3,0,2:T(8,128)} reduce(f32[2,2,1024,2,2,1,256]{2,6,4,1,3,5,0:T(8,128)} %all_to_all.5, f32[]{:T(128)} %constant.21.clone.1), dimensions={0,5}, to_apply=%region_1.2 | reduce | flops 2097152 | bytes 25165828 | tf_op jit(solution)/shard_map/reduce_sum | solution.py:22
  250.5 8.7 %copy.29 = f32[2,1024,2,2,256]{4,1,0,3,2:T(8,128)} copy(f32[2,1024,2,2,256]{1,4,3,0,2:T(8,128)} %reduce_sum.9) | data formatting | bytes 16777216 | tf_op jit(solution)/shard_map/reduce_sum | solution.py:22
  259.2 5.4 %slice_bitcast_fusion.3 = (f32[512,4,256]{2,0,1:T(8,128)}, f32[512,4,256]{2,0,1:T(8,128)}, f32[1,512,4,256]{3,1,2,0:T(8,128)S(1)}) fusion(f32[4,512,4,256]{3,1,0,2:T(8,128)} %bitcast.69), kind=kLoop, calls=%fused_computation.11 | loop fusion | bytes 12582912 | tf_op jit(solution)/shard_map/squeeze | solution.py:33
  264.6 4.7 %collective-permute-start = (f32[512,4,256]{2,0,1:T(8,128)}, f32[512,4,256]{2,0,1:T(8,128)}, u32[]{:S(2)}, u32[]{:S(2)}) collective-permute-start(f32[512,4,256]{2,0,1:T(8,128)} %get-tuple-element.12), channel_id=1, source_target_pairs={{0,16},{16,32},{32,48},{48,64},{64,80},{80,96},{96,112},{1,17},{17... | collective-permute-start | bytes 6291464 | tf_op jit(solution)/shard_map/ppermute | solution.py:28
  269.3 1.9 collective-permute-start.1
  271.2 2.5 bitcast_select_fusion.3
  273.7 41.0 %collective-permute-done = f32[512,4,256]{2,0,1:T(8,128)} collective-permute-done((f32[512,4,256]{2,0,1:T(8,128)}, f32[512,4,256]{2,0,1:T(8,128)}, u32[]{:S(2)}, u32[]{:S(2)}) %collective-permute-start) | collective-permute-done | bytes 2097184 | tf_op jit(solution)/shard_map/ppermute | solution.py:28
  314.8 7.7 %collective-permute-done.1 = f32[512,4,256]{2,0,1:T(8,128)} collective-permute-done((f32[512,4,256]{2,0,1:T(8,128)}, f32[512,4,256]{2,0,1:T(8,128)}, u32[]{:S(2)}, u32[]{:S(2)}) %collective-permute-start.1) | collective-permute-done | bytes 2097184 | tf_op jit(solution)/shard_map/ppermute | solution.py:28
  322.5 4.2 %fusion.6 = (f32[1,512,4,256]{3,1,2,0:T(8,128)S(1)}, f32[1,512,4,256]{3,1,2,0:T(8,128)S(1)}) fusion(f32[512,4,256]{2,0,1:T(8,128)} %collective-permute-done, f32[4,512,4,256]{3,1,0,2:T(8,128)} %bitcast.71, pred[]{:T(512)S(6)} %eq.18, f32[512,4,256]{2,0,1:T(8,128)} %collective-permute-done.1, pred[]{:T(512)S(6)} %eq.20), kind=kLoop, calls=%fused_computation.16 | loop fusion | flops 1048576 | bytes 12582914 | tf_op jit(solution)/shard_map/stack | solution.py:94
  326.7 1.0 pad_maximum_fusion
  327.8 3.0 slice_bitcast_fusion.1
  330.8 1.6 copy-done
  332.4 3.3 collective-permute-start.2
  335.7 2.5 collective-permute-start.3
  338.3 2.5 bitcast_select_fusion.1
  340.8 40.3 %collective-permute-done.2 = f32[4,512,256]{2,1,0:T(8,128)} collective-permute-done((f32[4,512,256]{2,1,0:T(8,128)}, f32[4,512,256]{2,1,0:T(8,128)}, u32[]{:S(2)}, u32[]{:S(2)}) %collective-permute-start.2) | collective-permute-done | bytes 2097184 | tf_op jit(solution)/shard_map/ppermute | solution.py:28
  381.1 5.1 %collective-permute-done.3 = f32[4,512,256]{2,1,0:T(8,128)} collective-permute-done((f32[4,512,256]{2,1,0:T(8,128)}, f32[4,512,256]{2,1,0:T(8,128)}, u32[]{:S(2)}, u32[]{:S(2)}) %collective-permute-start.3) | collective-permute-done | bytes 2097184 | tf_op jit(solution)/shard_map/ppermute | solution.py:28
  386.3 4.2 %fusion.5 = (f32[4,512,1,256]{3,1,0,2:T(8,128)S(1)}, f32[4,512,1,256]{3,1,0,2:T(8,128)S(1)}) fusion(f32[4,512,256]{2,1,0:T(8,128)} %collective-permute-done.2, f32[4,512,4,256]{3,1,2,0:T(8,128)} %copy-done, pred[]{:T(512)S(6)} %eq.17, f32[4,512,256]{2,1,0:T(8,128)} %collective-permute-done.3, pred[]{:T(512)S(6)} %eq.21), kind=kLoop, calls=%fused_computation.13 | loop fusion | flops 1048576 | bytes 12582914 | tf_op jit(solution)/shard_map/stack | solution.py:98
  390.5 3.7 pad_maximum_fusion.1
  394.2 12.2 %copy.38 = f32[4,512,4,256]{3,2,1,0:T(4,128)} copy(f32[4,512,4,256]{3,1,0,2:T(8,128)} %pad_maximum_fusion.1) | data formatting | bytes 16777216 | tf_op jit(solution)/shard_map/stack | solution.py:98
  (3 shorter events, 0.0 us)
Async XLA Ops:
  6.5 55.6 %all-gather.3.cloned.1.call-start = ((), (), s32[]{:S(2)}) async-start(), calls=%async_computation.2 | async-start | bytes 8912896 | tf_op jit(solution)/shard_map/all_gather | solution.py:68
  7.3 177.9 %all-reduce.2.cloned.1.call-start = ((), (), s32[]{:S(2)}) async-start(), calls=%async_computation.1 | async-start | bytes 8388608 | tf_op jit(solution)/shard_map/psum | solution.py:11
  264.6 50.2 %collective-permute-start = (f32[512,4,256]{2,0,1:T(8,128)}, f32[512,4,256]{2,0,1:T(8,128)}, u32[]{:S(2)}, u32[]{:S(2)}) collective-permute-start(f32[512,4,256]{2,0,1:T(8,128)} %get-tuple-element.12), channel_id=1, source_target_pairs={{0,16},{16,32},{32,48},{48,64},{64,80},{80,96},{96,112},{1,17},{17... | collective-permute-start | bytes 6291464 | tf_op jit(solution)/shard_map/ppermute | solution.py:28
  269.3 53.2 %collective-permute-start.1 = (f32[512,4,256]{2,0,1:T(8,128)}, f32[512,4,256]{2,0,1:T(8,128)}, u32[]{:S(2)}, u32[]{:S(2)}) collective-permute-start(f32[512,4,256]{2,0,1:T(8,128)} %get-tuple-element.13), channel_id=1, source_target_pairs={{16,0},{32,16},{48,32},{64,48},{80,64},{96,80},{112,96},{17,1},{33... | collective-permute-start | bytes 6291464 | tf_op jit(solution)/shard_map/ppermute | solution.py:28
  327.7 4.7 %copy-start = (f32[4,512,4,256]{3,1,2,0:T(8,128)}, f32[4,512,4,256]{3,1,2,0:T(8,128)S(1)}, u32[]{:S(2)}) copy-start(f32[4,512,4,256]{3,1,2,0:T(8,128)S(1)} %pad_maximum_fusion) | copy-start | bytes 25165828
  332.4 48.7 %collective-permute-start.2 = (f32[4,512,256]{2,1,0:T(8,128)}, f32[4,512,256]{2,1,0:T(8,128)}, u32[]{:S(2)}, u32[]{:S(2)}) collective-permute-start(f32[4,512,256]{2,1,0:T(8,128)} %get-tuple-element.7), channel_id=1, source_target_pairs={{0,2},{2,4},{4,6},{6,8},{8,10},{10,12},{12,14},{1,3},{3,5},{5,7},{... | collective-permute-start | bytes 6291464 | tf_op jit(solution)/shard_map/ppermute | solution.py:28
  335.7 50.6 %collective-permute-start.3 = (f32[4,512,256]{2,1,0:T(8,128)}, f32[4,512,256]{2,1,0:T(8,128)}, u32[]{:S(2)}, u32[]{:S(2)}) collective-permute-start(f32[4,512,256]{2,1,0:T(8,128)} %get-tuple-element.8), channel_id=1, source_target_pairs={{2,0},{4,2},{6,4},{8,6},{10,8},{12,10},{14,12},{3,1},{5,3},{7,5},{... | collective-permute-start | bytes 6291464 | tf_op jit(solution)/shard_map/ppermute | solution.py:28
Sparse Core Ops, SparseCore 0:
  9.0 53.0 all-gather.2
  77.0 108.1 all-reduce.1
where the time goes:
time: 414 us; the launch traced here: 413 us
  waiting for transfers between devices  216 us (52%)
  matrix products  62.6 us (15%)
  local copies, waits for them, and re-layouts  54.7 us (13%)
  other arithmetic  34.9 us (8%)
  blocking collectives  19 us (5%)
  between operations  13.5 us (3%)
  starting transfers between devices  12.5 us (3%)
    ppermute x4, waiting for transfers between devices, passed_along(): return lax.ppermute(block, axis, route)  94.2 us
    psum x1, waiting for transfers between devices, broadcast(): return lax.psum(jnp.where(mine, x, jnp.zeros_like(x)), axis)  66.1 us
    all_gather x1, waiting for transfers between devices, shards(): lax.all_gather(transforms[0], ('col', 'layer'), axis=1, tiled=True)  54.8 us
    dot_general x1, matrix products, shards(): jnp.einsum('pka,pkc->pac', left_panel, grouped, precision=exact_mode, pre...  31.5 us
    dot_general x1, matrix products, shards(): jnp.einsum('paqmh,qmhb->paqb', partial_rows, right_part, precision=exact_...  31.1 us
    all_to_all x1, blocking collectives, sum_at_owner(): blocks = lax.all_to_all(cut_along(x, dim, count), axis, 0, 0, tiled=True)  19 us
    ppermute x4, starting transfers between devices, passed_along(): return lax.ppermute(block, axis, route)  12.5 us
    reduce_sum x1, other arithmetic, sum_at_owner(): return jnp.sum(blocks, axis=0)  12.2 us
  transfers between devices with their start and end apart: 6, of which 6 were waited for; matrix products, arithmetic and copies ran while one was open for 11% of the time, Pallas kernels for 0%

commit v1 on v0

--- a/solution.py
+++ b/solution.py
@@ -8,7 +8,7 @@
 
 def broadcast(x, axis, root):
     mine = lax.axis_index(axis) == root
-    return lax.psum(jnp.where(mine, x, jnp.zeros_like(x)), axis)
+    return jnp.sum(lax.all_gather(jnp.where(mine, x, jnp.zeros_like(x)), axis), axis=0)
 
 
 def cut_along(x, dim, count):

time: 414 us -> 644 us (1.56)
  waiting for transfers between devices: 216 us -> 439 us
  other arithmetic: 34.9 us -> 49.9 us
  local copies, waits for them, and re-layouts: 54.7 us -> 44.5 us
    all_gather x0 -> x1, waiting for transfers between devices: none -> 290 us  [broadcast(): lax.all_gather(jnp.where(mine, x, jnp.zeros_like(x)), axis)]
    psum x1 -> x0, waiting for transfers between devices: 66.1 us -> none  [broadcast(): return lax.psum(jnp.where(mine, x, jnp.zeros_like(x)), axis)]
    reduce_sum x0 -> x1, other arithmetic: none -> 14.7 us  [broadcast(): jnp.sum(lax.all_gather(jnp.where(mine, x, jnp.zeros_like(x)), axis), axis=0)]
  transfers between devices with their start and end apart: 6 -> 6, of which waited for: 6 -> 6; matrix products, arithmetic and copies ran while one was open for 11% -> 8% of each run, Pallas kernels for 0% -> 0%
where the time goes in v1:
time: 644 us; the launch traced here: 643 us
  waiting for transfers between devices  439 us (68%)
  matrix products  64.5 us (10%)
  other arithmetic  49.9 us (8%)
  local copies, waits for them, and re-layouts  44.5 us (7%)
  blocking collectives  19 us (3%)
  between operations  13.5 us (2%)
  starting transfers between devices  12.4 us (2%)
    all_gather x1, waiting for transfers between devices, broadcast(): lax.all_gather(jnp.where(mine, x, jnp.zeros_like(x)), axis)  290 us
    ppermute x4, waiting for transfers between devices, passed_along(): return lax.ppermute(block, axis, route)  94 us
    all_gather x1, waiting for transfers between devices, shards(): lax.all_gather(transforms[0], ('col', 'layer'), axis=1, tiled=True)  54.8 us
    dot_general x1, matrix products, shards(): jnp.einsum('pka,pkc->pac', left_panel, grouped, precision=exact_mode, pre...  33 us
    dot_general x1, matrix products, shards(): jnp.einsum('paqmh,qmhb->paqb', partial_rows, right_part, precision=exact_...  31.5 us
    all_to_all x1, blocking collectives, sum_at_owner(): blocks = lax.all_to_all(cut_along(x, dim, count), axis, 0, 0, tiled=True)  19 us
    reduce_sum x1, other arithmetic, broadcast(): jnp.sum(lax.all_gather(jnp.where(mine, x, jnp.zeros_like(x)), axis), axis=0)  14.7 us
  transfers between devices with their start and end apart: 6, of which 6 were waited for; matrix products, arithmetic and copies ran while one was open for 8% of the time, Pallas kernels for 0%

profile of v1, /device:TPU:120, one launch (start us, length us, event | category | flops | bytes accessed | tf_op | source)
XLA Modules:
  0.0 643.0 jit_solution(15843240598117510296)
XLA Ops:
  6.5 0.7 all-gather.5.cloned.1.call-update
  7.3 0.0 all-gather.7.cloned.1.call-start
  7.3 54.8 %all-gather.5.cloned.1.call-done = f32[1,2,1024,1024]{3,2,1,0:T(8,128)} async-done(((f32[1,2,64,1024]{3,2,1,0:T(8,128)}), f32[1,2,1024,1024]{3,2,1,0:T(8,128)}) %all-gather.5.cloned.1.call-update) | async-done | bytes 8388624 | tf_op jit(solution)/shard_map/all_gather | solution.py:68
  62.1 5.1 dynamic-slice_select_fusion
  67.2 0.0 all-gather.7.cloned.1.call-update
  67.2 10.7 %reshape.15 = f32[2,1024,1024]{2,1,0:T(8,128)} reshape(f32[4,512,4,256]{3,2,1,0:T(4,128)} %param.2) | data formatting | bytes 16777216 | tf_op jit(solution)/shard_map/reshape | solution.py:72
  78.0 33.0 %fusion.2 = f32[2,1024,1024]{1,2,0:T(8,128)} fusion(f32[2,1024,1024]{2,1,0:T(8,128)} %reshape.15, f32[1,2,1024,1024]{3,2,1,0:T(8,128)} %all-gather.5.cloned.1.call-done), kind=kOutput, calls=%fused_computation.5 | convolution fusion | flops 25769803776 | bytes 25165824 | tf_op jit(solution)/shard_map/pka,pkc->pac/dot_general | solution.py:73
  110.9 289.6 %all-gather.7.cloned.1.call-done = f32[16,2,256,1024]{3,2,1,0:T(8,128)} async-done(((f32[2,2,256,1024]{3,2,1,0:T(8,128)}), f32[16,2,256,1024]{3,2,1,0:T(8,128)}) %all-gather.7.cloned.1.call-update) | async-done | bytes 33554448 | tf_op jit(solution)/shard_map/all_gather | solution.py:11
  400.5 14.7 %reduce_sum.18 = f32[2,2,256,1024]{3,2,1,0:T(8,128)} reduce(f32[8,2,2,256,1024]{4,3,2,1,0:T(8,128)} %bitcast.73, f32[]{:T(128)} %constant.21.clone.1), dimensions={0}, to_apply=%region_0.1 | reduce | flops 7340032 | bytes 37748740 | tf_op jit(solution)/shard_map/reduce_sum | solution.py:11
  415.2 31.5 %fusion = f32[2,1024,2,1024,1]{3,1,4,2,0:T(8,128)S(1)} fusion(f32[2,1024,2,2,256]{1,4,3,2,0:T(8,128)} %bitcast.74, f32[2,2,256,1024]{3,2,1,0:T(8,128)} %reduce_sum.18), kind=kOutput, calls=%fused_computation.3 | convolution fusion | flops 25769803776 | bytes 29360128 | tf_op jit(solution)/shard_map/paqmh,qmhb->paqb/dot_general | solution.py:81
  446.7 2.9 copy.54
  449.6 19.0 %all_to_all.5 = f32[2,2,1024,2,2,1,256]{2,6,4,1,3,5,0:T(8,128)} all-to-all(f32[2,2,1024,2,2,1,256]{2,6,4,1,3,5,0:T(8,128)S(1)} %bitcast.69), channel_id=1, replica_groups=mesh['row'=8,'col'=8,'layer'=2] {'layer'}, dimensions={0} | all-to-all | bytes 33554432 | tf_op jit(solution)/shard_map/all_to_all | solution.py:21
  468.6 12.2 %reduce_sum.19 = f32[2,1024,2,2,256]{1,4,3,0,2:T(8,128)} reduce(f32[2,2,1024,2,2,1,256]{2,6,4,1,3,5,0:T(8,128)} %all_to_all.5, f32[]{:T(128)} %constant.21.clone.1), dimensions={0,5}, to_apply=%region_1.2 | reduce | flops 2097152 | bytes 25165828 | tf_op jit(solution)/shard_map/reduce_sum | solution.py:22
  480.8 8.7 %copy.27 = f32[2,1024,2,2,256]{4,1,0,3,2:T(8,128)} copy(f32[2,1024,2,2,256]{1,4,3,0,2:T(8,128)} %reduce_sum.19) | data formatting | bytes 16777216 | tf_op jit(solution)/shard_map/reduce_sum | solution.py:22
  489.5 5.4 slice_bitcast_fusion.3
  494.9 4.4 collective-permute-start
  499.3 2.1 collective-permute-start.1
  501.5 2.5 bitcast_select_fusion.3
  504.0 40.8 %collective-permute-done = f32[512,4,256]{2,0,1:T(8,128)} collective-permute-done((f32[512,4,256]{2,0,1:T(8,128)}, f32[512,4,256]{2,0,1:T(8,128)}, u32[]{:S(2)}, u32[]{:S(2)}) %collective-permute-start) | collective-permute-done | bytes 2097184 | tf_op jit(solution)/shard_map/ppermute | solution.py:28
  544.8 7.7 %collective-permute-done.1 = f32[512,4,256]{2,0,1:T(8,128)} collective-permute-done((f32[512,4,256]{2,0,1:T(8,128)}, f32[512,4,256]{2,0,1:T(8,128)}, u32[]{:S(2)}, u32[]{:S(2)}) %collective-permute-start.1) | collective-permute-done | bytes 2097184 | tf_op jit(solution)/shard_map/ppermute | solution.py:28
  552.5 4.2 fusion.6
  556.7 0.8 pad_maximum_fusion
  557.6 3.0 slice_bitcast_fusion.1
  560.6 1.6 copy-done
  562.2 3.3 collective-permute-start.2
  565.5 2.5 collective-permute-start.3
  568.1 2.5 bitcast_select_fusion.1
  570.6 40.3 %collective-permute-done.2 = f32[4,512,256]{2,1,0:T(8,128)} collective-permute-done((f32[4,512,256]{2,1,0:T(8,128)}, f32[4,512,256]{2,1,0:T(8,128)}, u32[]{:S(2)}, u32[]{:S(2)}) %collective-permute-start.2) | collective-permute-done | bytes 2097184 | tf_op jit(solution)/shard_map/ppermute | solution.py:28
  610.9 5.1 collective-permute-done.3
  616.1 4.2 fusion.5
  620.3 3.7 pad_maximum_fusion.1
  624.0 12.2 %copy.36 = f32[4,512,4,256]{3,2,1,0:T(4,128)} copy(f32[4,512,4,256]{3,1,0,2:T(8,128)} %pad_maximum_fusion.1) | data formatting | bytes 16777216 | tf_op jit(solution)/shard_map/stack | solution.py:98
  (2 shorter events, 0.0 us)
Async XLA Ops:
  6.5 55.6 %all-gather.5.cloned.1.call-start = ((), (), s32[]{:S(2)}) async-start(), calls=%async_computation.1 | async-start | bytes 8912896 | tf_op jit(solution)/shard_map/all_gather | solution.py:68
  7.3 393.2 %all-gather.7.cloned.1.call-start = ((), (), s32[]{:S(2)}) async-start(), calls=%async_computation.2 | async-start | bytes 37748736 | tf_op jit(solution)/shard_map/all_gather | solution.py:11
  494.9 49.9 %collective-permute-start = (f32[512,4,256]{2,0,1:T(8,128)}, f32[512,4,256]{2,0,1:T(8,128)}, u32[]{:S(2)}, u32[]{:S(2)}) collective-permute-start(f32[512,4,256]{2,0,1:T(8,128)} %get-tuple-element.12), channel_id=1, source_target_pairs={{0,16},{16,32},{32,48},{48,64},{64,80},{80,96},{96,112},{1,17},{17... | collective-permute-start | bytes 6291464 | tf_op jit(solution)/shard_map/ppermute | solution.py:28
  499.3 53.2 %collective-permute-start.1 = (f32[512,4,256]{2,0,1:T(8,128)}, f32[512,4,256]{2,0,1:T(8,128)}, u32[]{:S(2)}, u32[]{:S(2)}) collective-permute-start(f32[512,4,256]{2,0,1:T(8,128)} %get-tuple-element.13), channel_id=1, source_target_pairs={{16,0},{32,16},{48,32},{64,48},{80,64},{96,80},{112,96},{17,1},{33... | collective-permute-start | bytes 6291464 | tf_op jit(solution)/shard_map/ppermute | solution.py:28
  557.5 4.7 copy-start
  562.2 48.7 %collective-permute-start.2 = (f32[4,512,256]{2,1,0:T(8,128)}, f32[4,512,256]{2,1,0:T(8,128)}, u32[]{:S(2)}, u32[]{:S(2)}) collective-permute-start(f32[4,512,256]{2,1,0:T(8,128)} %get-tuple-element.7), channel_id=1, source_target_pairs={{0,2},{2,4},{4,6},{6,8},{8,10},{10,12},{12,14},{1,3},{3,5},{5,7},{... | collective-permute-start | bytes 6291464 | tf_op jit(solution)/shard_map/ppermute | solution.py:28
  565.5 50.6 %collective-permute-start.3 = (f32[4,512,256]{2,1,0:T(8,128)}, f32[4,512,256]{2,1,0:T(8,128)}, u32[]{:S(2)}, u32[]{:S(2)}) collective-permute-start(f32[4,512,256]{2,1,0:T(8,128)} %get-tuple-element.8), channel_id=1, source_target_pairs={{2,0},{4,2},{6,4},{8,6},{10,8},{12,10},{14,12},{3,1},{5,3},{7,5},{... | collective-permute-start | bytes 6291464 | tf_op jit(solution)/shard_map/ppermute | solution.py:28
Sparse Core Ops, SparseCore 0:
  9.0 53.0 all-gather.4
  67.4 333.0 all-gather.6
